TPU v7x, 32 devices: a whole 2x2x4 slice. The times are simulated.
32 devices in a mesh: job: 2 (over y), slab: 16 (over z, x, core).
Axes of the slice: x: 2, y: 2, z: 4, core: 2. Of those that a mesh axis runs over, the one named last changes fastest.
Arguments:
- partials: bfloat16 [8, 32, 256, 256], P('job', None, 'slab'), parts along dimension 0, may hold values from -1.5 to 1.5
- regions: int32 [64, 256, 256], P(('job', 'slab')), parts along dimension 0, may hold values from 0 to 2
- previous: float32 [64, 256, 256], P(('job', 'slab')), parts along dimension 0, may hold values from -6 to 6
Outputs:
- potential: float32 [64, 256, 256], P(('job', 'slab')), parts along dimension 0
There are 2 independent parts, one for each index of `job`. A program takes and returns all parts, laid end to end along the dimension named above; each array names one. Nothing has to cross between parts.
Inputs may be any that keep to these rules, and one draw needn't show every extreme that they name: `regions`: 0 marks the solute's interior, 1 the ion-free solvent layer, 2 bulk solvent.
All inputs are finite; a program needn't handle non-finite values.
Results may differ from a plain program's by a relative error of at most 0.0003.
Values sent between devices are 32-bit elements; how exact they have to be, the bound alone decides.
A program may use at most 256 MiB of HBM per device.

v0:
```python
import jax
import jax.numpy as jnp
from jax import lax
from jax.sharding import PartitionSpec as P

PRE_SWEEPS = 2
POST_SWEEPS = 2
COARSE_SWEEPS = 4


DAMPING = 0.75
INSIDE = 2.0
SOLVENT = 78.4
SCREEN = 1.4
SOURCE = 16.0 * 3.141592653589793


def extended(cells, sides, width):
    for axis, dim in sides:
        count = lax.axis_size(axis)
        ends = count - 1
        head = lax.slice_in_dim(cells, 0, width, axis=dim)
        tail = lax.slice_in_dim(cells, cells.shape[dim] - width, cells.shape[dim], axis=dim)
        cells = jnp.concatenate(
            [
                lax.ppermute(tail, axis, [(i, (i + 1) % count) for i in range(ends)]),
                cells,
                lax.ppermute(head, axis, [((i + 1) % count, i) for i in range(ends)]),
            ],
            axis=dim,
        )
    return cells


def from_behind(value, axis, steps):
    count = lax.axis_size(axis)
    initial, last = (max(0, -steps), min(count, count - steps))
    return lax.ppermute(value, axis, [(source, source + steps) for source in range(initial, last)])


def partner_2(value, axis, apart):
    return lax.ppermute(value, axis, [(i, i ^ 1 << apart) for i in range(lax.axis_size(axis))])


def pad_plane(values):
    return jnp.pad(values, ((0, 0), (1, 1), (1, 1)))


def shifted_views(padded):
    return (
        padded[:-2, 1:-1, 1:-1],
        padded[2:, 1:-1, 1:-1],
        padded[1:-1, :-2, 1:-1],
        padded[1:-1, 2:, 1:-1],
        padded[1:-1, 1:-1, :-2],
        padded[1:-1, 1:-1, 2:],
    )


def face_coefficients(padded, spacing_z, spacing_x):
    centre = padded[1:-1, 1:-1, 1:-1]
    spacings = (spacing_z, spacing_z, spacing_x, spacing_x, spacing_x, spacing_x)
    result = []
    for neighbour, spacing in zip(shifted_views(padded), spacings):
        facing = jnp.where(neighbour > 0.0, neighbour, centre)
        result.append(2.0 * centre * facing / ((centre + facing) * spacing))
    return tuple(result)


def diagonal_of(coefficients, screening):
    running = coefficients[0]
    for coefficient in coefficients[1:]:
        running = running + coefficient
    return running + screening


def beside_sum(coefficients, padded):
    neighbours = shifted_views(padded)
    running = coefficients[0] * neighbours[0]
    for position in range(1, 6):
        running = running + coefficients[position] * neighbours[position]
    return running


def ghost_planes(stacked, layout, group_size, devices):
    if layout == "local":
        return extended(stacked, (("slab", 1),), 1)
    if layout == "group" and group_size < devices:
        lower_rim = from_behind(stacked, "slab", group_size)
        upper_rim = from_behind(stacked, "slab", -group_size)
        return jnp.concatenate([lower_rim, stacked, upper_rim], axis=1)
    return jnp.pad(stacked, ((0, 0), (1, 1), (0, 0), (0, 0)))


def remainder(source_term, solution, coefficients, diagonal, layout, group_size, devices):
    padded = ghost_planes(solution[None], layout, group_size, devices)[0]
    return source_term - diagonal * solution + beside_sum(coefficients, pad_plane(padded))


def coarsen(stacked):
    members = stacked.shape[0]
    planes = stacked.shape[1]
    plane_width = stacked.shape[2]
    blocks = stacked.reshape(members, planes // 2, 2, plane_width // 2, 2, plane_width // 2, 2)
    return jnp.mean(blocks, axis=(2, 4, 6))


def refine(values, double_z):
    if double_z:
        values = jnp.repeat(values, 2, axis=0)
    values = jnp.repeat(jnp.repeat(values, 2, axis=1), 2, axis=2)
    return values


def v_cycle(
    layout, group_size, devices, source_term, dielectric, screening, initial, spacing_z, spacing_x
):
    planes = source_term.shape[0]
    if initial is None:
        padded_diel = ghost_planes(dielectric[None], layout, group_size, devices)[0]
    else:
        stacked_pair = ghost_planes(jnp.stack([initial, dielectric]), layout, group_size, devices)
        padded_diel = stacked_pair[1]
    coefficients = face_coefficients(pad_plane(padded_diel), spacing_z, spacing_x)
    diagonal = diagonal_of(coefficients, screening)
    coarsest = planes == 1 and (layout == "full" or group_size == devices)
    sweeps = COARSE_SWEEPS if coarsest else PRE_SWEEPS
    if initial is None:
        solution = DAMPING * source_term / diagonal
    else:
        rest = (
            source_term - diagonal * initial + beside_sum(coefficients, pad_plane(stacked_pair[0]))
        )
        solution = initial + DAMPING * rest / diagonal
    for sweep_index in range(sweeps - 1):
        rest = remainder(source_term, solution, coefficients, diagonal, layout, group_size, devices)
        solution = solution + DAMPING * rest / diagonal
    if coarsest:
        return solution
    residual = remainder(source_term, solution, coefficients, diagonal, layout, group_size, devices)
    next_x = spacing_x * 4.0
    stacked = jnp.stack([residual, dielectric, screening])
    if planes >= 2:
        coarse = coarsen(stacked)
        correction = v_cycle(
            layout,
            group_size,
            devices,
            coarse[0],
            coarse[1],
            coarse[2],
            None,
            spacing_z * 4.0,
            next_x,
        )
        correction = refine(correction, True)
    else:
        partner = partner_2(stacked, "slab", group_size.bit_length() - 1)
        upper_half = lax.axis_index("slab") // group_size % 2
        merged = jnp.where(
            upper_half == 0,
            jnp.concatenate([stacked, partner], axis=1),
            jnp.concatenate([partner, stacked], axis=1),
        )
        coarse = coarsen(merged)
        merged_size = group_size * 2
        correction = v_cycle(
            "group",
            merged_size,
            devices,
            coarse[0],
            coarse[1],
            coarse[2],
            None,
            spacing_z * 4.0,
            next_x,
        )
        correction = refine(correction, False)
    solution = solution + correction
    for sweep_index in range(POST_SWEEPS):
        rest = remainder(source_term, solution, coefficients, diagonal, layout, group_size, devices)
        solution = solution + DAMPING * rest / diagonal
    return solution


def local(partials, regions, previous):
    devices = lax.axis_size("slab")
    density = jnp.sum(partials, axis=0, dtype=jnp.float32)
    slab_data = lax.all_to_all(density, "slab", split_axis=0, concat_axis=1, tiled=True)
    source_term = SOURCE * slab_data
    dielectric = jnp.where(regions == 0, INSIDE, SOLVENT).astype(jnp.float32)
    screening = jnp.where(regions == 2, SCREEN, 0.0).astype(jnp.float32)
    return v_cycle("local", 1, devices, source_term, dielectric, screening, previous, 1.0, 1.0)


def solution(mesh):
    in_specs = (
        P("job", None, "slab", None),
        P(("job", "slab"), None, None),
        P(("job", "slab"), None, None),
    )
    out_specs = P(("job", "slab"), None, None)
    return jax.shard_map(local, mesh=mesh, in_specs=in_specs, out_specs=out_specs, check_vma=False)
```

profile of v0, /device:TPU:9, one launch (start us, length us, event | category | flops | bytes accessed | tf_op | source)
XLA Modules:
  0.0 529.5 jit_solution(8208558791871034702)
XLA Ops:
  3.4 3.7 collective-permute-start
  9.9 6.5 %all-to-all-start = ((f32[32,16,256]{2,1,0:T(8,128)}), f32[32,16,256]{2,1,0:T(8,128)S(1)}, u32[]{:S(2)}, u32[]{:S(2)}) async-start(f32[32,16,256]{2,1,0:T(8,128)} %convert_reduce_fusion), calls=%async_computation | async-start | bytes 1048576 | tf_op jit(solution)/shard_map/all_to_all | solution.py:189
  16.5 4.0 collective-permute-done
  23.2 7.4 %all-to-all-done = f32[32,16,256]{2,1,0:T(8,128)S(1)} async-done(((f32[32,16,256]{2,1,0:T(8,128)}), f32[32,16,256]{2,1,0:T(8,128)S(1)}, u32[]{:S(2)}, u32[]{:S(2)}) %all-to-all-start) | async-done | bytes 524320 | tf_op jit(solution)/shard_map/all_to_all | solution.py:189
  40.7 4.6 collective-permute-done.3
  51.7 35.6 %stack.77 = f32[1,1,2,128,2,128,2]{6,5,4,3,2,1,0:T(8,128)} reshape(f32[2,256,256]{2,1,0:T(8,128)} %get-tuple-element.57) | data formatting | bytes 1048576 | tf_op jit(solution)/shard_map/stack | solution.py:142
  87.3 35.7 %stack.78 = f32[1,1,2,128,2,128,2]{6,5,4,3,2,1,0:T(8,128)} reshape(f32[2,256,256]{2,1,0:T(8,128)} %get-tuple-element.40) | data formatting | bytes 1048576 | tf_op jit(solution)/shard_map/stack | solution.py:142
  124.1 3.0 fusion.43
  127.1 35.6 %stack.76 = f32[1,1,2,128,2,128,2]{6,5,4,3,2,1,0:T(8,128)} reshape(f32[2,256,256]{2,1,0:T(8,128)} %fusion.43) | data formatting | bytes 1048576 | tf_op jit(solution)/shard_map/stack | solution.py:142
  162.7 31.5 %maximum_reduce_fusion = f32[3,128,128]{2,1,0:T(8,128)} fusion(f32[1,1,2,128,2,128,2]{6,5,4,3,2,1,0:T(8,128)} %stack.78, f32[1,1,2,128,2,128,2]{6,5,4,3,2,1,0:T(8,128)} %stack.77, f32[1,1,2,128,2,128,2]{6,5,4,3,2,1,0:T(8,128)} %stack.76), kind=kLoop, calls=%fused_computation | loop fusion | flops 1130496 | bytes 1769472 | tf_op jit(solution)/shard_map/reduce_sum | solution.py:105
  195.1 4.1 collective-permute-start.6
  201.2 3.6 collective-permute-done.7
  209.5 4.9 collective-permute-done.9
  219.7 3.2 collective-permute-done.11
  223.8 10.6 %stack.81 = f32[2,1,1,64,2,64,2]{6,5,4,3,0,2,1:T(8,128)} reshape(f32[2,128,128]{2,1,0:T(8,128)} %get-tuple-element.59) | data formatting | bytes 262144 | tf_op jit(solution)/shard_map/stack | solution.py:142
  234.4 6.1 %copy.101 = f32[2,1,1,64,2,64,2]{5,3,6,4,2,1,0:T(8,128)} copy(f32[2,1,1,64,2,64,2]{6,5,4,3,0,2,1:T(8,128)} %stack.81) | data formatting | bytes 262144 | tf_op jit(solution)/shard_map/stack | solution.py:142
  240.4 6.3 %stack.80 = f32[1,1,1,64,2,64,2]{6,5,4,3,2,1,0:T(8,128)} reshape(f32[1,128,128]{2,1,0:T(8,128)} %copy-done.25) | data formatting | bytes 131072 | tf_op jit(solution)/shard_map/stack | solution.py:142
  246.7 3.6 copy.100
  250.3 14.7 %concatenate.216 = f32[3,1,1,64,2,64,2]{6,5,4,3,0,2,1:T(8,128)} reshape(f32[3,1,128,128]{3,2,0,1:T(8,128)} %collective-permute-done.12) | data formatting | bytes 393216 | tf_op jit(solution)/shard_map/concatenate | solution.py:162
  265.0 8.5 %copy.102 = f32[3,1,1,64,2,64,2]{5,3,6,4,2,1,0:T(8,128)} copy(f32[3,1,1,64,2,64,2]{6,5,4,3,0,2,1:T(8,128)} %concatenate.216) | data formatting | bytes 393216 | tf_op jit(solution)/shard_map/concatenate | solution.py:162
  275.2 4.2 collective-permute-start.13
  284.2 2.9 collective-permute-start.15
  287.1 3.3 collective-permute-start.16
  294.7 3.7 collective-permute-start.18
  301.2 4.3 stack.86
  305.5 3.1 copy.106
  308.6 2.8 stack.85
  313.7 5.1 concatenate.222
  318.8 3.4 copy.107
  325.5 3.4 collective-permute-start.21
  332.0 3.4 collective-permute-start.23
  338.6 3.6 collective-permute-start.25
  361.0 4.0 collective-permute-done.28
  368.1 4.0 collective-permute-done.30
  375.7 3.4 collective-permute-done.32
  396.2 4.2 collective-permute-start.34
  401.8 4.0 collective-permute-done.35
  409.6 4.0 collective-permute-done.37
  421.8 3.4 collective-permute-start.39
  429.2 3.3 collective-permute-start.41
  441.4 3.7 collective-permute-start.43
  447.1 3.4 collective-permute-start.44
  450.5 3.1 collective-permute-start.45
  462.1 22.6 %collective-permute-start.46 = (f32[1,1,128,128]{3,2,1,0:T(8,128)S(1)}, f32[1,1,128,128]{3,2,1,0:T(8,128)S(1)}, u32[]{:S(2)}, u32[]{:S(2)}) collective-permute-start(f32[1,1,128,128]{3,2,1,0:T(8,128)S(1)} %bitcast.483), channel_id=1, source_target_pairs={{0,1},{1,2},{2,3},{3,4},{4,5},{5,6},{6,7},{7,8},{8,9},{9,10},{10,1... | collective-permute-start | bytes 196616 | tf_op jit(solution)/shard_map/ppermute | solution.py:26
  486.7 3.6 collective-permute-done.47
  495.8 3.2 collective-permute-done.49
  509.2 6.3 %collective-permute-done.51 = f32[1,1,256,256]{3,2,1,0:T(8,128)S(1)} collective-permute-done((f32[1,1,256,256]{3,2,1,0:T(8,128)S(1)}, f32[1,1,256,256]{3,2,1,0:T(8,128)S(1)}, u32[]{:S(2)}, u32[]{:S(2)}) %collective-permute-start.51) | collective-permute-done | bytes 262176 | tf_op jit(solution)/shard_map/ppermute | solution.py:28
  522.1 5.3 %collective-permute-done.53 = f32[1,1,256,256]{3,2,1,0:T(8,128)S(1)} collective-permute-done((f32[1,1,256,256]{3,2,1,0:T(8,128)S(1)}, f32[1,1,256,256]{3,2,1,0:T(8,128)S(1)}, u32[]{:S(2)}, u32[]{:S(2)}) %collective-permute-start.53) | collective-permute-done | bytes 262176 | tf_op jit(solution)/shard_map/ppermute | solution.py:28
  (293 shorter events, 170.5 us)
Async XLA Ops:
  3.4 17.1 %collective-permute-start = (f32[2,1,256,256]{3,2,1,0:T(8,128)}, f32[2,1,256,256]{3,2,1,0:T(8,128)S(1)}, u32[]{:S(2)}, u32[]{:S(2)}) collective-permute-start(f32[2,1,256,256]{3,2,1,0:T(8,128)} %get-tuple-element.47), channel_id=1, source_target_pairs={{0,1},{1,2},{2,3},{3,4},{4,5},{5,6},{6,7},{7,8},{8,9},{9,10},{10,1... | collective-permute-start | bytes 1572872 | tf_op jit(solution)/shard_map/ppermute | solution.py:26
  7.0 14.9 %collective-permute-start.1 = (f32[2,1,256,256]{3,2,1,0:T(8,128)S(1)}, f32[2,1,256,256]{3,2,1,0:T(8,128)S(1)}, u32[]{:S(2)}, u32[]{:S(2)}) collective-permute-start(f32[2,1,256,256]{3,2,1,0:T(8,128)S(1)} %get-tuple-element.48), channel_id=1, source_target_pairs={{1,0},{2,1},{3,2},{4,3},{5,4},{6,5},{7,6},{8,7},{9,8},{10,9},{11,1... | collective-permute-start | bytes 1572872 | tf_op jit(solution)/shard_map/ppermute | solution.py:28
  9.9 20.7 %all-to-all-start = ((f32[32,16,256]{2,1,0:T(8,128)}), f32[32,16,256]{2,1,0:T(8,128)S(1)}, u32[]{:S(2)}, u32[]{:S(2)}) async-start(f32[32,16,256]{2,1,0:T(8,128)} %convert_reduce_fusion), calls=%async_computation | async-start | bytes 1048576 | tf_op jit(solution)/shard_map/all_to_all | solution.py:189
  34.7 5.9 %collective-permute-start.2 = (f32[1,1,256,256]{3,2,1,0:T(8,128)S(1)}, f32[1,1,256,256]{3,2,1,0:T(8,128)S(1)}, u32[]{:S(2)}, u32[]{:S(2)}) collective-permute-start(f32[1,1,256,256]{3,2,1,0:T(8,128)S(1)} %get-tuple-element.55), channel_id=1, source_target_pairs={{0,1},{1,2},{2,3},{3,4},{4,5},{5,6},{6,7},{7,8},{8,9},{9,10},{10,1... | collective-permute-start | bytes 786440 | tf_op jit(solution)/shard_map/ppermute | solution.py:26
  37.4 7.9 %collective-permute-start.3 = (f32[1,1,256,256]{3,2,1,0:T(8,128)S(1)}, f32[1,1,256,256]{3,2,1,0:T(8,128)S(1)}, u32[]{:S(2)}, u32[]{:S(2)}) collective-permute-start(f32[1,1,256,256]{3,2,1,0:T(8,128)S(1)} %get-tuple-element.56), channel_id=1, source_target_pairs={{1,0},{2,1},{3,2},{4,3},{5,4},{6,5},{7,6},{8,7},{9,8},{10,9},{11,1... | collective-permute-start | bytes 786440 | tf_op jit(solution)/shard_map/ppermute | solution.py:28
  47.4 75.6 %collective-permute-start.4 = (f32[1,1,256,256]{3,2,1,0:T(8,128)}, f32[1,1,256,256]{3,2,1,0:T(8,128)}, u32[]{:S(2)}, u32[]{:S(2)}) collective-permute-start(f32[1,1,256,256]{3,2,1,0:T(8,128)} %get-tuple-element.53), channel_id=1, source_target_pairs={{0,1},{1,2},{2,3},{3,4},{4,5},{5,6},{6,7},{7,8},{8,9},{9,10},{10,1... | collective-permute-start | bytes 786440 | tf_op jit(solution)/shard_map/ppermute | solution.py:26
  49.3 73.7 %collective-permute-start.5 = (f32[1,1,256,256]{3,2,1,0:T(8,128)}, f32[1,1,256,256]{3,2,1,0:T(8,128)}, u32[]{:S(2)}, u32[]{:S(2)}) collective-permute-start(f32[1,1,256,256]{3,2,1,0:T(8,128)} %get-tuple-element.54), channel_id=1, source_target_pairs={{1,0},{2,1},{3,2},{4,3},{5,4},{6,5},{7,6},{8,7},{9,8},{10,9},{11,1... | collective-permute-start | bytes 786440 | tf_op jit(solution)/shard_map/ppermute | solution.py:28
  195.1 6.0 %collective-permute-start.6 = (f32[1,1,128,128]{3,2,1,0:T(8,128)S(1)}, f32[1,1,128,128]{3,2,1,0:T(8,128)S(1)}, u32[]{:S(2)}, u32[]{:S(2)}) collective-permute-start(f32[1,1,128,128]{3,2,1,0:T(8,128)S(1)} %slice_bitcast_fusion.2), channel_id=1, source_target_pairs={{0,1},{1,2},{2,3},{3,4},{4,5},{5,6},{6,7},{7,8},{8,9},{9,10},{10,1... | collective-permute-start | bytes 196616 | tf_op jit(solution)/shard_map/ppermute | solution.py:26
  199.2 5.6 %collective-permute-start.7 = (f32[1,1,128,128]{3,2,1,0:T(8,128)S(1)}, f32[1,1,128,128]{3,2,1,0:T(8,128)S(1)}, u32[]{:S(2)}, u32[]{:S(2)}) collective-permute-start(f32[1,1,128,128]{3,2,1,0:T(8,128)S(1)} %slice_bitcast_fusion.2), channel_id=1, source_target_pairs={{1,0},{2,1},{3,2},{4,3},{5,4},{6,5},{7,6},{8,7},{9,8},{10,9},{11,1... | collective-permute-start | bytes 196616 | tf_op jit(solution)/shard_map/ppermute | solution.py:28
  207.0 7.4 %collective-permute-start.9 = (f32[1,1,128,128]{3,2,1,0:T(8,128)S(1)}, f32[1,1,128,128]{3,2,1,0:T(8,128)S(1)}, u32[]{:S(2)}, u32[]{:S(2)}) collective-permute-start(f32[1,1,128,128]{3,2,1,0:T(8,128)S(1)} %get-tuple-element.31), channel_id=1, source_target_pairs={{1,0},{2,1},{3,2},{4,3},{5,4},{6,5},{7,6},{8,7},{9,8},{10,9},{11,1... | collective-permute-start | bytes 196616 | tf_op jit(solution)/shard_map/ppermute | solution.py:28
  214.5 5.2 collective-permute-start.10
  216.4 6.5 %collective-permute-start.11 = (f32[1,1,128,128]{3,2,1,0:T(8,128)S(1)}, f32[1,1,128,128]{3,2,1,0:T(8,128)S(1)}, u32[]{:S(2)}, u32[]{:S(2)}) collective-permute-start(f32[1,1,128,128]{3,2,1,0:T(8,128)S(1)} %bitcast.480), channel_id=1, source_target_pairs={{1,0},{2,1},{3,2},{4,3},{5,4},{6,5},{7,6},{8,7},{9,8},{10,9},{11,1... | collective-permute-start | bytes 196616 | tf_op jit(solution)/shard_map/ppermute | solution.py:28
  223.8 26.6 %collective-permute-start.12 = (f32[3,1,128,128]{3,2,0,1:T(8,128)}, f32[3,1,128,128]{3,2,0,1:T(8,128)}, u32[]{:S(2)}, u32[]{:S(2)}) collective-permute-start(f32[3,1,128,128]{3,2,0,1:T(8,128)} %pad_maximum_fusion.14), channel_id=1, source_target_pairs={{0,1},{1,0},{2,3},{3,2},{4,5},{5,4},{6,7},{7,6},{8,9},{9,8},{10,11... | collective-permute-start | bytes 589832 | tf_op jit(solution)/shard_map/ppermute | solution.py:42
  275.2 6.2 %collective-permute-start.13 = (f32[1,1,64,64]{3,2,1,0:T(8,128)S(1)}, f32[1,1,64,64]{3,2,1,0:T(8,128)S(1)}, u32[]{:S(2)}, u32[]{:S(2)}) collective-permute-start(f32[1,1,64,64]{3,2,1,0:T(8,128)S(1)} %slice_bitcast_fusion.3), channel_id=1, source_target_pairs={{0,2},{1,3},{2,4},{3,5},{4,6},{5,7},{6,8},{7,9},{8,10},{9,11},{10,... | collective-permute-start | bytes 49160 | tf_op jit(solution)/shard_map/ppermute | solution.py:38
  279.4 4.7 collective-permute-start.14
  284.2 6.2 %collective-permute-start.15 = (f32[1,1,64,64]{3,2,1,0:T(8,128)S(1)}, f32[1,1,64,64]{3,2,1,0:T(8,128)S(1)}, u32[]{:S(2)}, u32[]{:S(2)}) collective-permute-start(f32[1,1,64,64]{3,2,1,0:T(8,128)S(1)} %get-tuple-element.24), channel_id=1, source_target_pairs={{0,2},{1,3},{2,4},{3,5},{4,6},{5,7},{6,8},{7,9},{8,10},{9,11},{10,... | collective-permute-start | bytes 49160 | tf_op jit(solution)/shard_map/ppermute | solution.py:38
  287.1 5.0 collective-permute-start.16
  292.2 6.8 %collective-permute-start.17 = (f32[1,1,64,64]{3,2,1,0:T(8,128)S(1)}, f32[1,1,64,64]{3,2,1,0:T(8,128)S(1)}, u32[]{:S(2)}, u32[]{:S(2)}) collective-permute-start(f32[1,1,64,64]{3,2,1,0:T(8,128)S(1)} %bitcast.490), channel_id=1, source_target_pairs={{0,2},{1,3},{2,4},{3,5},{4,6},{5,7},{6,8},{7,9},{8,10},{9,11},{10,... | collective-permute-start | bytes 49160 | tf_op jit(solution)/shard_map/ppermute | solution.py:38
  294.7 4.7 collective-permute-start.18
  300.2 13.5 %collective-permute-start.19 = (f32[3,1,64,64]{3,2,0,1:T(8,128)}, f32[3,1,64,64]{3,2,0,1:T(8,128)}, u32[]{:S(2)}, u32[]{:S(2)}) collective-permute-start(f32[3,1,64,64]{3,2,0,1:T(8,128)} %pad_maximum_fusion.15), channel_id=1, source_target_pairs={{0,2},{1,3},{2,0},{3,1},{4,6},{5,7},{6,4},{7,5},{8,10},{9,11},{10,... | collective-permute-start | bytes 147464 | tf_op jit(solution)/shard_map/ppermute | solution.py:42
  323.5 5.3 %collective-permute-start.20 = (f32[1,1,32,32]{3,2,1,0:T(8,128)S(1)}, f32[1,1,32,32]{3,2,1,0:T(8,128)S(1)}, u32[]{:S(2)}, u32[]{:S(2)}) collective-permute-start(f32[1,1,32,32]{3,2,1,0:T(8,128)S(1)} %slice_bitcast_fusion.4), channel_id=1, source_target_pairs={{0,4},{1,5},{2,6},{3,7},{4,8},{5,9},{6,10},{7,11},{8,12},{9,13},{1... | collective-permute-start | bytes 12296 | tf_op jit(solution)/shard_map/ppermute | solution.py:38
  325.5 4.5 collective-permute-start.21
  330.1 5.3 %collective-permute-start.22 = (f32[1,1,32,32]{3,2,1,0:T(8,128)S(1)}, f32[1,1,32,32]{3,2,1,0:T(8,128)S(1)}, u32[]{:S(2)}, u32[]{:S(2)}) collective-permute-start(f32[1,1,32,32]{3,2,1,0:T(8,128)S(1)} %get-tuple-element.17), channel_id=1, source_target_pairs={{0,4},{1,5},{2,6},{3,7},{4,8},{5,9},{6,10},{7,11},{8,12},{9,13},{1... | collective-permute-start | bytes 12296 | tf_op jit(solution)/shard_map/ppermute | solution.py:38
  332.0 4.5 collective-permute-start.23
  336.6 6.1 %collective-permute-start.24 = (f32[1,1,32,32]{3,2,1,0:T(8,128)S(1)}, f32[1,1,32,32]{3,2,1,0:T(8,128)S(1)}, u32[]{:S(2)}, u32[]{:S(2)}) collective-permute-start(f32[1,1,32,32]{3,2,1,0:T(8,128)S(1)} %bitcast.502), channel_id=1, source_target_pairs={{0,4},{1,5},{2,6},{3,7},{4,8},{5,9},{6,10},{7,11},{8,12},{9,13},{1... | collective-permute-start | bytes 12296 | tf_op jit(solution)/shard_map/ppermute | solution.py:38
  338.6 4.5 collective-permute-start.25
  343.8 8.9 %collective-permute-start.26 = (f32[3,1,32,32]{3,2,0,1:T(8,128)}, f32[3,1,32,32]{3,2,0,1:T(8,128)}, u32[]{:S(2)}, u32[]{:S(2)}) collective-permute-start(f32[3,1,32,32]{3,2,0,1:T(8,128)} %pad_maximum_fusion.16), channel_id=1, source_target_pairs={{0,4},{1,5},{2,6},{3,7},{4,0},{5,1},{6,2},{7,3},{8,12},{9,13},{10,... | collective-permute-start | bytes 36872 | tf_op jit(solution)/shard_map/ppermute | solution.py:42
  359.7 5.3 collective-permute-start.28
  366.8 5.3 collective-permute-start.30
  373.8 5.3 collective-permute-start.32
  379.9 6.4 %collective-permute-start.33 = (f32[3,1,16,16]{3,2,0,1:T(8,128)}, f32[3,1,16,16]{3,2,0,1:T(8,128)}, u32[]{:S(2)}, u32[]{:S(2)}) collective-permute-start(f32[3,1,16,16]{3,2,0,1:T(8,128)} %pad_maximum_fusion.17), channel_id=1, source_target_pairs={{0,8},{1,9},{2,10},{3,11},{4,12},{5,13},{6,14},{7,15},{8,0},{9,1},... | collective-permute-start | bytes 9224 | tf_op jit(solution)/shard_map/ppermute | solution.py:42
  396.2 5.5 %collective-permute-start.34 = (f32[1,1,16,16]{3,2,1,0:T(8,128)S(1)}, f32[1,1,16,16]{3,2,1,0:T(8,128)S(1)}, u32[]{:S(2)}, u32[]{:S(2)}) collective-permute-start(f32[1,1,16,16]{3,2,1,0:T(8,128)S(1)} %bitcast.518), channel_id=1, source_target_pairs={{0,8},{1,9},{2,10},{3,11},{4,12},{5,13},{6,14},{7,15},{16,24},{17,... | collective-permute-start | bytes 3080 | tf_op jit(solution)/shard_map/ppermute | solution.py:38
  400.5 5.3 collective-permute-start.35
  408.3 5.3 collective-permute-start.37
  419.9 5.3 collective-permute-start.38
  421.8 4.5 collective-permute-start.39
  427.2 5.3 %collective-permute-start.40 = (f32[1,1,32,32]{3,2,1,0:T(8,128)S(1)}, f32[1,1,32,32]{3,2,1,0:T(8,128)S(1)}, u32[]{:S(2)}, u32[]{:S(2)}) collective-permute-start(f32[1,1,32,32]{3,2,1,0:T(8,128)S(1)} %bitcast.509), channel_id=1, source_target_pairs={{0,4},{1,5},{2,6},{3,7},{4,8},{5,9},{6,10},{7,11},{8,12},{9,13},{1... | collective-permute-start | bytes 12296 | tf_op jit(solution)/shard_map/ppermute | solution.py:38
  438.9 6.2 %collective-permute-start.42 = (f32[1,1,64,64]{3,2,1,0:T(8,128)S(1)}, f32[1,1,64,64]{3,2,1,0:T(8,128)S(1)}, u32[]{:S(2)}, u32[]{:S(2)}) collective-permute-start(f32[1,1,64,64]{3,2,1,0:T(8,128)S(1)} %bitcast.494), channel_id=1, source_target_pairs={{0,2},{1,3},{2,4},{3,5},{4,6},{5,7},{6,8},{7,9},{8,10},{9,11},{10,... | collective-permute-start | bytes 49160 | tf_op jit(solution)/shard_map/ppermute | solution.py:38
  441.4 4.7 collective-permute-start.43
  447.1 6.5 %collective-permute-start.44 = (f32[1,1,64,64]{3,2,1,0:T(8,128)S(1)}, f32[1,1,64,64]{3,2,1,0:T(8,128)S(1)}, u32[]{:S(2)}, u32[]{:S(2)}) collective-permute-start(f32[1,1,64,64]{3,2,1,0:T(8,128)S(1)} %bitcast.497), channel_id=1, source_target_pairs={{0,2},{1,3},{2,4},{3,5},{4,6},{5,7},{6,8},{7,9},{8,10},{9,11},{10,... | collective-permute-start | bytes 49160 | tf_op jit(solution)/shard_map/ppermute | solution.py:38
  450.5 4.7 collective-permute-start.45
  462.1 24.5 %collective-permute-start.46 = (f32[1,1,128,128]{3,2,1,0:T(8,128)S(1)}, f32[1,1,128,128]{3,2,1,0:T(8,128)S(1)}, u32[]{:S(2)}, u32[]{:S(2)}) collective-permute-start(f32[1,1,128,128]{3,2,1,0:T(8,128)S(1)} %bitcast.483), channel_id=1, source_target_pairs={{0,1},{1,2},{2,3},{3,4},{4,5},{5,6},{6,7},{7,8},{8,9},{9,10},{10,1... | collective-permute-start | bytes 196616 | tf_op jit(solution)/shard_map/ppermute | solution.py:26
  484.7 5.6 %collective-permute-start.47 = (f32[1,1,128,128]{3,2,1,0:T(8,128)S(1)}, f32[1,1,128,128]{3,2,1,0:T(8,128)S(1)}, u32[]{:S(2)}, u32[]{:S(2)}) collective-permute-start(f32[1,1,128,128]{3,2,1,0:T(8,128)S(1)} %bitcast.484), channel_id=1, source_target_pairs={{1,0},{2,1},{3,2},{4,3},{5,4},{6,5},{7,6},{8,7},{9,8},{10,9},{11,1... | collective-permute-start | bytes 196616 | tf_op jit(solution)/shard_map/ppermute | solution.py:28
  493.4 5.6 %collective-permute-start.49 = (f32[1,1,128,128]{3,2,1,0:T(8,128)S(1)}, f32[1,1,128,128]{3,2,1,0:T(8,128)S(1)}, u32[]{:S(2)}, u32[]{:S(2)}) collective-permute-start(f32[1,1,128,128]{3,2,1,0:T(8,128)S(1)} %bitcast.487), channel_id=1, source_target_pairs={{1,0},{2,1},{3,2},{4,3},{5,4},{6,5},{7,6},{8,7},{9,8},{10,9},{11,1... | collective-permute-start | bytes 196616 | tf_op jit(solution)/shard_map/ppermute | solution.py:28
  504.0 5.2 collective-permute-start.50
  505.9 9.6 %collective-permute-start.51 = (f32[1,1,256,256]{3,2,1,0:T(8,128)S(1)}, f32[1,1,256,256]{3,2,1,0:T(8,128)S(1)}, u32[]{:S(2)}, u32[]{:S(2)}) collective-permute-start(f32[1,1,256,256]{3,2,1,0:T(8,128)S(1)} %get-tuple-element.52), channel_id=1, source_target_pairs={{1,0},{2,1},{3,2},{4,3},{5,4},{6,5},{7,6},{8,7},{9,8},{10,9},{11,1... | collective-permute-start | bytes 786440 | tf_op jit(solution)/shard_map/ppermute | solution.py:28
  516.9 5.2 collective-permute-start.52
  518.8 8.6 %collective-permute-start.53 = (f32[1,1,256,256]{3,2,1,0:T(8,128)S(1)}, f32[1,1,256,256]{3,2,1,0:T(8,128)S(1)}, u32[]{:S(2)}, u32[]{:S(2)}) collective-permute-start(f32[1,1,256,256]{3,2,1,0:T(8,128)S(1)} %get-tuple-element.50), channel_id=1, source_target_pairs={{1,0},{2,1},{3,2},{4,3},{5,4},{6,5},{7,6},{8,7},{9,8},{10,9},{11,1... | collective-permute-start | bytes 786440 | tf_op jit(solution)/shard_map/ppermute | solution.py:28
  (50 other events, 634.2 us)
where the time goes:
time: 535 us; the launch traced here: 529 us
  local copies, waits for them, and re-layouts  227 us (42%)
  starting transfers between devices  151 us (28%)
  waiting for transfers between devices  81.7 us (15%)
  other arithmetic  68.1 us (13%)
    another operation x19, local copies, waits for them, and re-layouts, v_cycle(): stacked = jnp.stack([residual, dielectric, screening])  160 us
    ppermute x30, starting transfers between devices, from_behind(): lax.ppermute(value, axis, [(source, source + steps) for source in range(i...  74.8 us
    ppermute x10, starting transfers between devices, extended(): lax.ppermute(tail, axis, [(i, (i + 1) % count) for i in range(ends)])  44.5 us
    concatenate x8, local copies, waits for them, and re-layouts, v_cycle(): jnp.concatenate([stacked, partner], axis=1)  39.7 us
    reduce_sum x5, other arithmetic, coarsen(): return jnp.mean(blocks, axis=(2, 4, 6))  36.2 us
    ppermute x10, waiting for transfers between devices, extended(): lax.ppermute(head, axis, [((i + 1) % count, i) for i in range(ends)])  36.2 us
    ppermute x30, waiting for transfers between devices, from_behind(): lax.ppermute(value, axis, [(source, source + steps) for source in range(i...  31.2 us
    ppermute x10, starting transfers between devices, extended(): lax.ppermute(head, axis, [((i + 1) % count, i) for i in range(ends)])  22.7 us
  transfers between devices with their start and end apart: 55, of which 29 were waited for; matrix products, arithmetic and copies ran while one was open for 24% of the time, Pallas kernels for 0%

commit v1 on v0

v1 whole, which is shorter than its diff:
```python
import functools

import jax
import jax.numpy as jnp
from jax import lax
from jax.experimental import pallas as pl
from jax.experimental.pallas import tpu as pltpu
from jax.sharding import PartitionSpec as P

PRE_SWEEPS = 2
POST_SWEEPS = 2
COARSE_SWEEPS = 4

DAMPING = 0.75
INSIDE = 2.0
SOLVENT = 78.4
SCREEN = 1.4
SOURCE = 16.0 * 3.141592653589793

F32 = jnp.float32
LANES = 128


def iota(shape, dim):
    return lax.broadcasted_iota(jnp.int32, shape, dim)


def face(mine, other, spacing):
    return mine * other / ((mine + other) * (0.5 * spacing))


def back(v, dim, by=1):
    return pltpu.roll(v, by, dim)


def ahead(v, dim, by=1):
    return pltpu.roll(v, v.shape[dim] - by, dim)


def dot(a, b):
    return lax.dot_general(
        a, b, (((1,), (0,)), ((), ())),
        precision=lax.Precision.HIGHEST, preferred_element_type=F32)


def pool_right(wide, narrow, valid):
    src, dst = iota((wide, narrow), 0), iota((wide, narrow), 1)
    return jnp.where((src // 2 == dst) & (src < valid), 1.0, 0.0).astype(F32)


def pool_left(narrow, wide):
    dst, src = iota((narrow, wide), 0), iota((narrow, wide), 1)
    return jnp.where(src // 2 == dst, 1.0, 0.0).astype(F32)


def spread_right(narrow, wide, valid):
    src, dst = iota((narrow, wide), 0), iota((narrow, wide), 1)
    return jnp.where((dst // 2 == src) & (dst < valid), 1.0, 0.0).astype(F32)


def spread_left(wide, narrow):
    dst, src = iota((wide, narrow), 0), iota((wide, narrow), 1)
    return jnp.where(dst // 2 == src, 1.0, 0.0).astype(F32)


def plane_faces(e, spacing):
    rows, cols = e.shape
    x, y = iota(e.shape, 0), iota(e.shape, 1)
    fx = jnp.where(x > 0, face(e, back(e, 0), spacing), 0.0)
    fy = jnp.where(y > 0, face(e, back(e, 1), spacing), 0.0)
    edges = (jnp.where((x == 0) | (x == rows - 1), 1.0, 0.0)
             + jnp.where((y == 0) | (y == cols - 1), 1.0, 0.0))
    total = fx + ahead(fx, 0) + fy + ahead(fy, 1) + edges * e * (1.0 / spacing)
    return fx, fy, total


def plane_sum(fx, fy, v):
    return fx * back(v, 0) + ahead(fx * v, 0) + fy * back(v, 1) + ahead(fy * v, 1)


def coarse_cycle(b, e, k, planes, nx, sz, sx):
    rows = b.shape[0]
    row, lane = iota(b.shape, 0), iota(b.shape, 1)
    x, z = row % nx, row // nx
    valid = (row < planes * nx) & (lane < nx)
    e = jnp.where(valid, e, 1.0)
    fx = jnp.where(valid & (x > 0), face(e, back(e, 0), sx), 0.0) if nx > 1 else None
    fy = jnp.where(valid & (lane > 0), face(e, back(e, 1), sx), 0.0) if nx > 1 else None
    wrap = nx % rows
    fz = jnp.where(valid & (z > 0), face(e, back(e, 0, wrap), sz), 0.0) if planes > 1 else None
    diag = k + e * (
        (jnp.where(x == 0, 1.0, 0.0) + jnp.where(x == nx - 1, 1.0, 0.0)
         + jnp.where(lane == 0, 1.0, 0.0) + jnp.where(lane == nx - 1, 1.0, 0.0)) * (1.0 / sx)
        + (jnp.where(z == 0, 1.0, 0.0) + jnp.where(z == planes - 1, 1.0, 0.0)) * (1.0 / sz))
    if nx > 1:
        diag = diag + fx + ahead(fx, 0) + fy + ahead(fy, 1)
    if planes > 1:
        diag = diag + fz + ahead(fz, 0, wrap)
    w = jnp.where(valid, DAMPING / jnp.where(valid, diag, 1.0), 0.0)

    def beside(v):
        total = jnp.zeros_like(v)
        if nx > 1:
            total = plane_sum(fx, fy, v)
        if planes > 1:
            total = total + fz * back(v, 0, wrap) + ahead(fz * v, 0, wrap)
        return total

    def sweep(v):
        return (1.0 - DAMPING) * v + w * (b + beside(v))

    v = w * b
    for _ in range((COARSE_SWEEPS if planes == 1 else PRE_SWEEPS) - 1):
        v = sweep(v)
    if planes == 1:
        return v
    r = jnp.where(valid, b - diag * v + beside(v), 0.0)
    halve = nx > 1 and nx % 2 == 0
    nx2 = nx // 2 if halve else nx
    sx2 = sx * 4.0 if halve else sx
    step = planes
    while step * nx > 512 and step % 4 == 0:
        step //= 2
    part = step * nx
    if step == planes:
        part = rows
    real2 = planes // 2 * nx2
    rows2 = max(8, real2)
    part2 = rows2 if step == planes else step // 2 * nx2
    ratio = 2 if halve else 1

    def member(fine, coarse):
        return ((fine < step * nx) & ((fine // nx // 2) * nx2 + fine % nx // ratio == coarse))

    down = jnp.where(member(iota((part2, part), 1), iota((part2, part), 0)), 1.0, 0.0)
    up = jnp.where(member(iota((part, part2), 0), iota((part, part2), 1)), 1.0, 0.0)
    if halve:
        right = pool_right(LANES, LANES, nx)
        left = spread_right(LANES, LANES, nx)
        scale = 0.125
    else:
        scale = 0.5

    def coarsen(f):
        if halve:
            f = dot(f, right)
        parts = [dot(down, f[i:i + part]) for i in range(0, rows, part)]
        return scale * (parts[0] if len(parts) == 1 else jnp.concatenate(parts, axis=0))

    def refine(f):
        if halve:
            f = dot(f, left)
        parts = [dot(up, f[i:i + part2]) for i in range(0, rows2, part2)]
        return parts[0] if len(parts) == 1 else jnp.concatenate(parts, axis=0)

    c = coarse_cycle(coarsen(r), coarsen(jnp.where(valid, e, 0.0)), coarsen(k),
                     planes // 2, nx2, sz * 4.0, sx2)
    v = v + refine(c)
    for _ in range(POST_SWEEPS):
        v = sweep(v)
    return v


REG, V0, V1, V2, V3 = range(5)
E1, A1, A2, A3, A4 = range(5)


def kernel(n, partials, regions, previous, out,
           dens, got, b0, fx0, fy0, fz0, dg0, wt0, halo_reg, halo0, v1, v2, v3,
           halo1, plane1, gb, gk,
           big_send, big_recv, small_send, small_recv, many_send, many_recv, barrier_dummy):
    me = lax.axis_index("slab")
    job = lax.axis_index("job")
    nxy = regions.shape[1]
    half = nxy // 2
    quarter = nxy // 4
    rows = partials.shape[2]
    has_lo, has_hi = me > 0, me < n - 1

    def peer(index):
        return {"slab": index}

    barrier = pltpu.get_barrier_semaphore()

    def greet(off, carry):
        pl.semaphore_signal(barrier, inc=1, device_id=peer(lax.rem(me + off, n)),
                            device_id_type=pl.DeviceIdType.MESH)
        return carry

    lax.fori_loop(1, n, greet, 0)

    @pl.when(jnp.logical_not(has_lo))
    def _():
        for i in range(4):
            halo0[i, 0] = jnp.zeros((nxy, nxy), F32)
        for i in range(5):
            halo1[i, 0] = jnp.zeros((half, half), F32)
        halo_reg[0] = jnp.zeros((nxy, nxy), jnp.int32)

    @pl.when(jnp.logical_not(has_hi))
    def _():
        for i in range(4):
            halo0[i, 1] = jnp.zeros((nxy, nxy), F32)
        for i in range(5):
            halo1[i, 1] = jnp.zeros((half, half), F32)
        halo_reg[1] = jnp.zeros((nxy, nxy), jnp.int32)

    density = partials[0].astype(F32)
    for g in range(1, partials.shape[0]):
        density = density + partials[g].astype(F32)
    dens[...] = (SOURCE * density).reshape(dens.shape)

    pl.semaphore_wait(barrier, n - 1)

    def copies(first, last, dst, sends, recvs, i):
        to_lo = pltpu.make_async_remote_copy(
            src_ref=first, dst_ref=dst.at[1], send_sem=sends.at[i, 0], recv_sem=recvs.at[i, 1],
            device_id=peer(jnp.maximum(me - 1, 0)), device_id_type=pl.DeviceIdType.MESH)
        to_hi = pltpu.make_async_remote_copy(
            src_ref=last, dst_ref=dst.at[0], send_sem=sends.at[i, 1], recv_sem=recvs.at[i, 0],
            device_id=peer(jnp.minimum(me + 1, n - 1)), device_id_type=pl.DeviceIdType.MESH)

        def start():
            pl.when(has_lo)(to_lo.start)
            pl.when(has_hi)(to_hi.start)

        def recv():
            pl.when(has_lo)(to_hi.wait_recv)
            pl.when(has_hi)(to_lo.wait_recv)

        def sent():
            pl.when(has_lo)(to_lo.wait_send)
            pl.when(has_hi)(to_hi.wait_send)

        return start, recv, sent

    pending = []

    def launch(first, last, dst, sends, recvs, i):
        start, recv, sent = copies(first, last, dst, sends, recvs, i)
        start()
        pending.append(sent)
        return recv

    recv_reg = launch(regions.at[0], regions.at[1], halo_reg, big_send, big_recv, REG)
    recv_v0 = launch(previous.at[0], previous.at[1], halo0.at[0], big_send, big_recv, V0)

    def scatter(off, carry):
        other = lax.rem(me + off, n)
        pltpu.make_async_remote_copy(
            src_ref=dens.at[other], dst_ref=got.at[me], send_sem=many_send.at[0],
            recv_sem=many_recv.at[0], device_id=peer(other),
            device_id_type=pl.DeviceIdType.MESH).start()
        return carry

    lax.fori_loop(1, n, scatter, 0)

    def dielectric(r):
        return jnp.where(r == 0, INSIDE, SOLVENT).astype(F32)

    e = [dielectric(regions[p]) for p in range(2)]
    k = [jnp.where(regions[p] == 2, SCREEN, 0.0).astype(F32) for p in range(2)]
    right0, left0 = pool_right(nxy, half, nxy), pool_left(half, nxy)
    right1, left1 = pool_right(half, LANES, half), pool_left(quarter, half)

    def down0(a, b):
        return 0.125 * dot(left0, dot(a + b, right0))

    def down1(a):
        return 0.25 * dot(left1, dot(a, right1))

    e1, k1 = down0(e[0], e[1]), down0(k[0], k[1])
    plane1[E1] = e1
    recv_e1 = launch(plane1.at[E1], plane1.at[E1], halo1.at[E1], small_send, small_recv, E1)
    gk[me, 0] = down1(e1)
    gk[me, 1] = down1(k1)

    def share(ref, i):
        def one(off, carry):
            other = lax.rem(me + off, n)
            pltpu.make_async_remote_copy(
                src_ref=ref.at[me], dst_ref=ref.at[me], send_sem=many_send.at[i],
                recv_sem=many_recv.at[i], device_id=peer(other),
                device_id_type=pl.DeviceIdType.MESH).start()
            return carry

        lax.fori_loop(1, n, one, 0)

    def all_in(ref, sems, i):
        window = ref.at[pl.ds(0, n - 1)]
        pltpu.make_async_copy(window, window, sems.at[i]).wait()

    share(gk, 1)

    recv_reg()
    e_lo = jnp.where(has_lo, dielectric(halo_reg[0]), e[0])
    e_hi = jnp.where(has_hi, dielectric(halo_reg[1]), e[1])
    faces_z = [face(e_lo, e[0], 1.0), face(e[0], e[1], 1.0), face(e[1], e_hi, 1.0)]
    for i in range(3):
        fz0[i] = faces_z[i]
    for p in range(2):
        fx, fy, total = plane_faces(e[p], 1.0)
        fx0[p] = fx
        fy0[p] = fy
        total = total + faces_z[p] + faces_z[p + 1] + k[p]
        dg0[p] = total
        wt0[p] = DAMPING / total

    def beside0(p, mine, below, above):
        return plane_sum(fx0[p], fy0[p], mine) + fz0[p] * below + fz0[p + 1] * above

    recv_e1()
    sz1 = sx1 = 4.0
    fx1, fy1, total1 = plane_faces(e1, sx1)
    fz1lo = face(jnp.where(has_lo, halo1[E1, 0], e1), e1, sz1)
    fz1hi = face(jnp.where(has_hi, halo1[E1, 1], e1), e1, sz1)
    dg1 = total1 + fz1lo + fz1hi + k1
    wt1 = DAMPING / dg1

    def sweep0(p, mine, below, above):
        return (1.0 - DAMPING) * mine + wt0[p] * (b0[p] + beside0(p, mine, below, above))

    recv_v0()
    previous_planes = [previous[0], previous[1]]
    part = [
        (1.0 - DAMPING) * previous_planes[0]
        + wt0[0] * beside0(0, previous_planes[0], halo0[0, 0], previous_planes[1]),
        (1.0 - DAMPING) * previous_planes[1]
        + wt0[1] * beside0(1, previous_planes[1], previous_planes[0], halo0[0, 1])]
    for p in range(2):
        v1[p] = part[p]

    got[me] = dens[me]
    all_in(got, many_recv, 0)
    for p in range(2):
        if rows % 8 == 0:
            b0[p] = got[:, p].reshape(nxy, nxy)
        else:
            for s in range(n):
                b0[p, s * rows:(s + 1) * rows, :] = got[s, p]
    for p in range(2):
        v1[p] = v1[p] + wt0[p] * b0[p]
    recv = launch(v1.at[0], v1.at[1], halo0.at[1], big_send, big_recv, V1)
    recv()
    v2[0] = sweep0(0, v1[0], halo0[1, 0], v1[1])
    v2[1] = sweep0(1, v1[1], v1[0], halo0[1, 1])
    recv = launch(v2.at[0], v2.at[1], halo0.at[2], big_send, big_recv, V2)
    recv()
    r0 = b0[0] - dg0[0] * v2[0] + beside0(0, v2[0], halo0[2, 0], v2[1])
    r1 = b0[1] - dg0[1] * v2[1] + beside0(1, v2[1], v2[0], halo0[2, 1])
    b1 = down0(r0, r1)

    def beside1(mine, i):
        return plane_sum(fx1, fy1, mine) + fz1lo * halo1[i, 0] + fz1hi * halo1[i, 1]

    def trade1(value, i):
        plane1[i] = value
        launch(plane1.at[i], plane1.at[i], halo1.at[i], small_send, small_recv, i)()

    a = wt1 * b1
    trade1(a, A1)
    a = (1.0 - DAMPING) * a + wt1 * (b1 + beside1(a, A1))
    trade1(a, A2)
    gb[me] = down1(b1 - dg1 * a + beside1(a, A2))
    share(gb, 2)
    all_in(gk, many_recv, 1)
    pair = gk[...].reshape(n // 2, 2, 2, quarter, LANES)
    e2 = 0.5 * (pair[:, 0, 0] + pair[:, 1, 0]).reshape(n // 2 * quarter, LANES)
    k2 = 0.5 * (pair[:, 0, 1] + pair[:, 1, 1]).reshape(n // 2 * quarter, LANES)
    all_in(gb, many_recv, 2)
    pair = gb[...].reshape(n // 2, 2, quarter, LANES)
    b2 = 0.5 * (pair[:, 0] + pair[:, 1]).reshape(n // 2 * quarter, LANES)
    c2 = coarse_cycle(b2, e2, k2, n // 2, quarter, 16.0, 16.0)

    for i in range(n // 2):
        dens2 = c2[i * quarter:(i + 1) * quarter]
        barrier_dummy[i] = dens2
    grow_l, grow_r = spread_left(half, quarter), spread_right(LANES, half, half)

    def up1(index):
        return dot(grow_l, dot(barrier_dummy[index // 2], grow_r))

    halo1[A2, 0] = halo1[A2, 0] + jnp.where(has_lo, up1(jnp.maximum(me - 1, 0)), 0.0)
    halo1[A2, 1] = halo1[A2, 1] + jnp.where(has_hi, up1(jnp.minimum(me + 1, n - 1)), 0.0)
    a = a + up1(me)
    a = (1.0 - DAMPING) * a + wt1 * (b1 + beside1(a, A2))
    trade1(a, A3)
    a = (1.0 - DAMPING) * a + wt1 * (b1 + beside1(a, A3))
    trade1(a, A4)

    big_l, big_r = spread_left(nxy, half), spread_right(half, nxy, nxy)

    def up0(c):
        return dot(big_l, dot(c, big_r))

    mine = up0(a)
    below = halo0[2, 0] + up0(halo1[A4, 0])
    above = halo0[2, 1] + up0(halo1[A4, 1])
    w0, w1 = v2[0] + mine, v2[1] + mine
    v3[0] = sweep0(0, w0, below, w1)
    v3[1] = sweep0(1, w1, w0, above)
    recv = launch(v3.at[0], v3.at[1], halo0.at[3], big_send, big_recv, V3)
    recv()
    out[0] = sweep0(0, v3[0], halo0[3, 0], v3[1])
    out[1] = sweep0(1, v3[1], v3[0], halo0[3, 1])

    for sent in pending:
        sent()
    all_in(got, many_send, 0)
    all_in(gk, many_send, 1)
    all_in(gb, many_send, 2)


def local(partials, regions, previous):
    n = lax.axis_size("slab")
    nxy = regions.shape[1]
    half, quarter = nxy // 2, nxy // 4
    rows = partials.shape[2]
    vmem = lambda *shape: pltpu.VMEM(shape, F32)
    spec = pl.BlockSpec(memory_space=pltpu.VMEM)
    return pl.pallas_call(
        functools.partial(kernel, n),
        out_shape=jax.ShapeDtypeStruct(previous.shape, F32),
        in_specs=[spec] * 3,
        out_specs=spec,
        scratch_shapes=[
            vmem(n, 2, rows, nxy), vmem(n, 2, rows, nxy), vmem(2, nxy, nxy),
            vmem(2, nxy, nxy), vmem(2, nxy, nxy), vmem(3, nxy, nxy), vmem(2, nxy, nxy),
            vmem(2, nxy, nxy),
            pltpu.VMEM((2, nxy, nxy), jnp.int32), vmem(4, 2, nxy, nxy),
            vmem(2, nxy, nxy), vmem(2, nxy, nxy), vmem(2, nxy, nxy),
            vmem(5, 2, half, half), vmem(5, half, half),
            vmem(n, quarter, LANES), vmem(n, 2, quarter, LANES),
            pltpu.SemaphoreType.DMA((5, 2)), pltpu.SemaphoreType.DMA((5, 2)),
            pltpu.SemaphoreType.DMA((5, 2)), pltpu.SemaphoreType.DMA((5, 2)),
            pltpu.SemaphoreType.DMA((3,)), pltpu.SemaphoreType.DMA((3,)),
            vmem(n // 2, quarter, LANES),
        ],
        compiler_params=pltpu.CompilerParams(
            collective_id=0, has_side_effects=True, vmem_limit_bytes=60 * 1024 * 1024),
    )(partials, regions, previous)


def solution(mesh):
    in_specs = (
        P("job", None, "slab", None),
        P(("job", "slab"), None, None),
        P(("job", "slab"), None, None),
    )
    out_specs = P(("job", "slab"), None, None)
    return jax.shard_map(local, mesh=mesh, in_specs=in_specs, out_specs=out_specs, check_vma=False)
```

time: 535 us -> 100 us (0.19); the launches traced: 529 us -> 100 us
  local copies, waits for them, and re-layouts: 227 us -> 1.87 us
  starting transfers between devices: 151 us -> 0 us
  Pallas kernels: 0 us -> 98.3 us
  waiting for transfers between devices: 81.7 us -> 0 us
  other arithmetic: 68.1 us -> 0 us
    another operation x19 -> x0, local copies, waits for them, and re-layouts: 160 us -> none  [v_cycle(): stacked = jnp.stack([residual, dielectric, screening])]
    ppermute x54 -> x0, starting transfers between devices: 145 us -> none  [the longest x30 74.8 us: from_behind(): lax.ppermute(value, axis, [(source, source + steps) for source in range(i...]
    pallas_call x0 -> x1, Pallas kernels: none -> 98.3 us  [local(): pl.pallas_call(functools.partial(kernel, n), out_shape=jax.ShapeDtypeStru...]
    ppermute x54 -> x0, waiting for transfers between devices: 74.3 us -> none  [the longest x10 36.2 us: extended(): lax.ppermute(head, axis, [((i + 1) % count, i) for i in range(ends)])]
    concatenate x8 -> x0, local copies, waits for them, and re-layouts: 39.7 us -> none  [v_cycle(): jnp.concatenate([stacked, partner], axis=1)]
    reduce_sum x6 -> x0, other arithmetic: 37.2 us -> none  [the longest x5 36.2 us: coarsen(): return jnp.mean(blocks, axis=(2, 4, 6))]
    add x28 -> x0, other arithmetic: 21.8 us -> none  [the longest x18 12.8 us: v_cycle(): solution = solution + DAMPING * rest / diagonal]
    broadcast_in_dim x21 -> x0, local copies, waits for them, and re-layouts: 21.7 us -> none  [refine(): values = jnp.repeat(jnp.repeat(values, 2, axis=1), 2, axis=2)]
  transfers between devices with their start and end apart: 55 -> 0, of which waited for: 29 -> 0; matrix products, arithmetic and copies ran while one was open for 24% -> 0% of each run, Pallas kernels for 0% -> 0%
where the time goes in v1:
time: 100 us
  Pallas kernels  98.3 us (98%)
  local copies, waits for them, and re-layouts  1.87 us (2%)
    pallas_call x1, Pallas kernels, local(): pl.pallas_call(functools.partial(kernel, n), out_shape=jax.ShapeDtypeStru...  98.3 us

profile of v1, /device:TPU:9, one launch (start us, length us, event | category | flops | bytes accessed | tf_op | source)
XLA Modules:
  0.0 100.2 jit_solution(1003279211014237426)
XLA Ops:
  0.0 98.3 %shard_map.37 = f32[2,256,256]{2,1,0:T(8,128)} custom-call(bf16[4,32,16,256]{3,2,1,0:T(8,128)(2,1)} %partials.1, s32[2,256,256]{2,1,0:T(8,128)} %regions.1, f32[2,256,256]{2,1,0:T(8,128)} %previous.1), custom_call_target="tpu_custom_call" | custom-call | tf_op jit(solution)/shard_map/pallas_call | solution.py:421
  98.3 1.9 %copy.5 = f32[2,256,256]{2,1,0:T(8,128)} copy(f32[2,256,256]{2,1,0:T(8,128)} %shard_map.37) | data formatting | bytes 1048576

commit v2 on v1

--- a/solution.py
+++ b/solution.py
@@ -162,13 +162,13 @@
 
 
 REG, V0, V1, V2, V3 = range(5)
-E1, A1, A2, A3, A4 = range(5)
+E1, A1, A2, A3, A4, TERM = range(6)
 
 
 def kernel(n, partials, regions, previous, out,
            dens, got, b0, fx0, fy0, fz0, dg0, wt0, halo_reg, halo0, v1, v2, v3,
-           halo1, plane1, gb, gk,
-           big_send, big_recv, small_send, small_recv, many_send, many_recv, barrier_dummy):
+           halo1, plane1, term1, gb, gk,
+           big_send, big_recv, small_send, small_recv, many_send, many_recv, c2_planes):
     me = lax.axis_index("slab")
     job = lax.axis_index("job")
     nxy = regions.shape[1]
@@ -193,7 +193,7 @@
     def _():
         for i in range(4):
             halo0[i, 0] = jnp.zeros((nxy, nxy), F32)
-        for i in range(5):
+        for i in range(6):
             halo1[i, 0] = jnp.zeros((half, half), F32)
         halo_reg[0] = jnp.zeros((nxy, nxy), jnp.int32)
 
@@ -201,7 +201,7 @@
     def _():
         for i in range(4):
             halo0[i, 1] = jnp.zeros((nxy, nxy), F32)
-        for i in range(5):
+        for i in range(6):
             halo1[i, 1] = jnp.zeros((half, half), F32)
         halo_reg[1] = jnp.zeros((nxy, nxy), jnp.int32)
 
@@ -245,15 +245,15 @@
     recv_reg = launch(regions.at[0], regions.at[1], halo_reg, big_send, big_recv, REG)
     recv_v0 = launch(previous.at[0], previous.at[1], halo0.at[0], big_send, big_recv, V0)
 
-    def scatter(off, carry):
-        other = lax.rem(me + off, n)
+    def scatter(step, carry):
+        other = lax.rem(me + 1 + lax.rem(step + n // 2 - 1, n - 1), n)
         pltpu.make_async_remote_copy(
             src_ref=dens.at[other], dst_ref=got.at[me], send_sem=many_send.at[0],
             recv_sem=many_recv.at[0], device_id=peer(other),
             device_id_type=pl.DeviceIdType.MESH).start()
         return carry
 
-    lax.fori_loop(1, n, scatter, 0)
+    lax.fori_loop(0, n - 1, scatter, 0)
 
     def dielectric(r):
         return jnp.where(r == 0, INSIDE, SOLVENT).astype(F32)
@@ -272,19 +272,31 @@
     e1, k1 = down0(e[0], e[1]), down0(k[0], k[1])
     plane1[E1] = e1
     recv_e1 = launch(plane1.at[E1], plane1.at[E1], halo1.at[E1], small_send, small_recv, E1)
-    gk[me, 0] = down1(e1)
-    gk[me, 1] = down1(k1)
+    core, chip = lax.rem(me, 2), me // 2
+    gk[core, chip] = down1(e1) + back(down1(k1), 1, LANES // 2)
 
     def share(ref, i):
         def one(off, carry):
-            other = lax.rem(me + off, n)
+            other = lax.rem(me + 2 * off, n)
             pltpu.make_async_remote_copy(
-                src_ref=ref.at[me], dst_ref=ref.at[me], send_sem=many_send.at[i],
+                src_ref=ref.at[core, chip], dst_ref=ref.at[core, chip], send_sem=many_send.at[i],
                 recv_sem=many_recv.at[i], device_id=peer(other),
                 device_id_type=pl.DeviceIdType.MESH).start()
             return carry
 
-        lax.fori_loop(1, n, one, 0)
+        lax.fori_loop(1, n // 2, one, 0)
+
+    def relay(ref, i):
+        window = ref.at[0, pl.ds(0, n // 2 - 1)]
+        pltpu.make_async_copy(window, window, many_recv.at[i]).wait()
+        copy = pltpu.make_async_remote_copy(
+            src_ref=ref.at[core], dst_ref=ref.at[core], send_sem=many_send.at[i + 2],
+            recv_sem=many_recv.at[i + 2], device_id=peer(me + 1 - 2 * core),
+            device_id_type=pl.DeviceIdType.MESH)
+        copy.start()
+        pending.append(pltpu.make_async_copy(window, window, many_send.at[i]).wait)
+        pending.append(copy.wait_send)
+        return copy.wait_recv
 
     def all_in(ref, sems, i):
         window = ref.at[pl.ds(0, n - 1)]
@@ -344,11 +356,16 @@
     recv()
     v2[0] = sweep0(0, v1[0], halo0[1, 0], v1[1])
     v2[1] = sweep0(1, v1[1], v1[0], halo0[1, 1])
-    recv = launch(v2.at[0], v2.at[1], halo0.at[2], big_send, big_recv, V2)
-    recv()
-    r0 = b0[0] - dg0[0] * v2[0] + beside0(0, v2[0], halo0[2, 0], v2[1])
-    r1 = b0[1] - dg0[1] * v2[1] + beside0(1, v2[1], v2[0], halo0[2, 1])
+    term1[0] = 0.125 * dot(left0, dot(fz0[0] * v2[0], right0))
+    term1[1] = 0.125 * dot(left0, dot(fz0[2] * v2[1], right0))
+    recv_term = launch(term1.at[0], term1.at[1], halo1.at[TERM], small_send, small_recv, TERM)
+    recv_v2 = launch(v2.at[0], v2.at[1], halo0.at[2], big_send, big_recv, V2)
+    r0 = b0[0] - dg0[0] * v2[0] + plane_sum(fx0[0], fy0[0], v2[0]) + fz0[1] * v2[1]
+    r1 = b0[1] - dg0[1] * v2[1] + plane_sum(fx0[1], fy0[1], v2[1]) + fz0[1] * v2[0]
     b1 = down0(r0, r1)
+    recv_gk = relay(gk, 1)
+    recv_term()
+    b1 = b1 + halo1[TERM, 0] + halo1[TERM, 1]
 
     def beside1(mine, i):
         return plane_sum(fx1, fy1, mine) + fz1lo * halo1[i, 0] + fz1hi * halo1[i, 1]
@@ -361,24 +378,26 @@
     trade1(a, A1)
     a = (1.0 - DAMPING) * a + wt1 * (b1 + beside1(a, A1))
     trade1(a, A2)
-    gb[me] = down1(b1 - dg1 * a + beside1(a, A2))
+    full = down1(b1 - dg1 * a + beside1(a, A2))
+    gb[core, chip] = full[:quarter // 2] + back(full[quarter // 2:], 1, LANES // 2)
     share(gb, 2)
-    all_in(gk, many_recv, 1)
-    pair = gk[...].reshape(n // 2, 2, 2, quarter, LANES)
-    e2 = 0.5 * (pair[:, 0, 0] + pair[:, 1, 0]).reshape(n // 2 * quarter, LANES)
-    k2 = 0.5 * (pair[:, 0, 1] + pair[:, 1, 1]).reshape(n // 2 * quarter, LANES)
-    all_in(gb, many_recv, 2)
-    pair = gb[...].reshape(n // 2, 2, quarter, LANES)
-    b2 = 0.5 * (pair[:, 0] + pair[:, 1]).reshape(n // 2 * quarter, LANES)
+    recv_gk()
+    e2 = 0.5 * (gk[0] + gk[1]).reshape(n // 2 * quarter, LANES)
+    k2 = back(e2, 1, LANES // 2)
+    relay(gb, 2)()
+    packed = 0.5 * (gb[0] + gb[1]).reshape(n // 2 * quarter // 2, LANES)
+    split = (n // 2, quarter // 2, LANES)
+    b2 = jnp.concatenate(
+        [packed.reshape(split), back(packed, 1, LANES // 2).reshape(split)], axis=1
+    ).reshape(n // 2 * quarter, LANES)
     c2 = coarse_cycle(b2, e2, k2, n // 2, quarter, 16.0, 16.0)
 
     for i in range(n // 2):
-        dens2 = c2[i * quarter:(i + 1) * quarter]
-        barrier_dummy[i] = dens2
+        c2_planes[i] = c2[i * quarter:(i + 1) * quarter]
     grow_l, grow_r = spread_left(half, quarter), spread_right(LANES, half, half)
 
     def up1(index):
-        return dot(grow_l, dot(barrier_dummy[index // 2], grow_r))
+        return dot(grow_l, dot(c2_planes[index // 2], grow_r))
 
     halo1[A2, 0] = halo1[A2, 0] + jnp.where(has_lo, up1(jnp.maximum(me - 1, 0)), 0.0)
     halo1[A2, 1] = halo1[A2, 1] + jnp.where(has_hi, up1(jnp.minimum(me + 1, n - 1)), 0.0)
@@ -393,6 +412,7 @@
     def up0(c):
         return dot(big_l, dot(c, big_r))
 
+    recv_v2()
     mine = up0(a)
     below = halo0[2, 0] + up0(halo1[A4, 0])
     above = halo0[2, 1] + up0(halo1[A4, 1])
@@ -407,8 +427,6 @@
     for sent in pending:
         sent()
     all_in(got, many_send, 0)
-    all_in(gk, many_send, 1)
-    all_in(gb, many_send, 2)
 
 
 def local(partials, regions, previous):
@@ -429,11 +447,11 @@
             vmem(2, nxy, nxy),
             pltpu.VMEM((2, nxy, nxy), jnp.int32), vmem(4, 2, nxy, nxy),
             vmem(2, nxy, nxy), vmem(2, nxy, nxy), vmem(2, nxy, nxy),
-            vmem(5, 2, half, half), vmem(5, half, half),
-            vmem(n, quarter, LANES), vmem(n, 2, quarter, LANES),
+            vmem(6, 2, half, half), vmem(5, half, half), vmem(2, half, half),
+            vmem(2, n // 2, quarter // 2, LANES), vmem(2, n // 2, quarter, LANES),
             pltpu.SemaphoreType.DMA((5, 2)), pltpu.SemaphoreType.DMA((5, 2)),
-            pltpu.SemaphoreType.DMA((5, 2)), pltpu.SemaphoreType.DMA((5, 2)),
-            pltpu.SemaphoreType.DMA((3,)), pltpu.SemaphoreType.DMA((3,)),
+            pltpu.SemaphoreType.DMA((6, 2)), pltpu.SemaphoreType.DMA((6, 2)),
+            pltpu.SemaphoreType.DMA((5,)), pltpu.SemaphoreType.DMA((5,)),
             vmem(n // 2, quarter, LANES),
         ],
         compiler_params=pltpu.CompilerParams(

time: 100 us -> 83.3 us (0.83)
  Pallas kernels: 98.3 us -> 81.2 us
    pallas_call x1, Pallas kernels: 98.3 us -> 81.2 us  [local(): pl.pallas_call(functools.partial(kernel, n), out_shape=jax.ShapeDtypeStru...]
where the time goes in v2:
time: 83.3 us; the launch traced here: 83.1 us
  Pallas kernels  81.2 us (97%)
  local copies, waits for them, and re-layouts  1.87 us (2%)
    pallas_call x1, Pallas kernels, local(): pl.pallas_call(functools.partial(kernel, n), out_shape=jax.ShapeDtypeStru...  81.2 us
    unnamed x1, local copies, waits for them, and re-layouts  1.87 us

profile of v2, /device:TPU:9, one launch (start us, length us, event | category | flops | bytes accessed | tf_op | source)
XLA Modules:
  0.0 83.1 jit_solution(1437727372163608890)
XLA Ops:
  0.0 81.2 %shard_map.37 = f32[2,256,256]{2,1,0:T(8,128)} custom-call(bf16[4,32,16,256]{3,2,1,0:T(8,128)(2,1)} %partials.1, s32[2,256,256]{2,1,0:T(8,128)} %regions.1, f32[2,256,256]{2,1,0:T(8,128)} %previous.1), custom_call_target="tpu_custom_call" | custom-call | tf_op jit(solution)/shard_map/pallas_call | solution.py:439
  81.2 1.9 %copy.5 = f32[2,256,256]{2,1,0:T(8,128)} copy(f32[2,256,256]{2,1,0:T(8,128)} %shard_map.37) | data formatting | bytes 1048576

commit v3 on v2

--- a/solution.py
+++ b/solution.py
@@ -78,9 +78,9 @@
     return fx * back(v, 0) + ahead(fx * v, 0) + fy * back(v, 1) + ahead(fy * v, 1)
 
 
-def coarse_cycle(b, e, k, planes, nx, sz, sx):
-    rows = b.shape[0]
-    row, lane = iota(b.shape, 0), iota(b.shape, 1)
+def coarse_cycle(e, k, planes, nx, sz, sx):
+    rows = e.shape[0]
+    row, lane = iota(e.shape, 0), iota(e.shape, 1)
     x, z = row % nx, row // nx
     valid = (row < planes * nx) & (lane < nx)
     e = jnp.where(valid, e, 1.0)
@@ -106,15 +106,17 @@
             total = total + fz * back(v, 0, wrap) + ahead(fz * v, 0, wrap)
         return total
 
-    def sweep(v):
+    def sweep(v, b):
         return (1.0 - DAMPING) * v + w * (b + beside(v))
 
-    v = w * b
-    for _ in range((COARSE_SWEEPS if planes == 1 else PRE_SWEEPS) - 1):
-        v = sweep(v)
+    def coarsest(b):
+        v = w * b
+        for _ in range(COARSE_SWEEPS - 1):
+            v = sweep(v, b)
+        return v
+
     if planes == 1:
-        return v
-    r = jnp.where(valid, b - diag * v + beside(v), 0.0)
+        return coarsest
     halve = nx > 1 and nx % 2 == 0
     nx2 = nx // 2 if halve else nx
     sx2 = sx * 4.0 if halve else sx
@@ -153,20 +155,28 @@
         parts = [dot(up, f[i:i + part2]) for i in range(0, rows2, part2)]
         return parts[0] if len(parts) == 1 else jnp.concatenate(parts, axis=0)
 
-    c = coarse_cycle(coarsen(r), coarsen(jnp.where(valid, e, 0.0)), coarsen(k),
-                     planes // 2, nx2, sz * 4.0, sx2)
-    v = v + refine(c)
-    for _ in range(POST_SWEEPS):
-        v = sweep(v)
-    return v
-
-
-REG, V0, V1, V2, V3 = range(5)
+    below = coarse_cycle(coarsen(jnp.where(valid, e, 0.0)), coarsen(k),
+                         planes // 2, nx2, sz * 4.0, sx2)
+
+    def run(b):
+        v = w * b
+        for _ in range(PRE_SWEEPS - 1):
+            v = sweep(v, b)
+        r = jnp.where(valid, b - diag * v + beside(v), 0.0)
+        v = v + refine(below(coarsen(r)))
+        for _ in range(POST_SWEEPS):
+            v = sweep(v, b)
+        return v
+
+    return run
+
+
+REG, V0, V1, V2, BASE, FAR = range(6)
 E1, A1, A2, A3, A4, TERM = range(6)
 
 
 def kernel(n, partials, regions, previous, out,
-           dens, got, b0, fx0, fy0, fz0, dg0, wt0, halo_reg, halo0, v1, v2, v3,
+           dens, got, b0, fx0, fy0, fz0, dg0, wt0, halo_reg, far_reg, fxh, fyh, fzh, wth, halo0, v1, v2, base,
            halo1, plane1, term1, gb, gk,
            big_send, big_recv, small_send, small_recv, many_send, many_recv, c2_planes):
     me = lax.axis_index("slab")
@@ -196,6 +206,7 @@
         for i in range(6):
             halo1[i, 0] = jnp.zeros((half, half), F32)
         halo_reg[0] = jnp.zeros((nxy, nxy), jnp.int32)
+        far_reg[0] = jnp.zeros((nxy, nxy), jnp.int32)
 
     @pl.when(jnp.logical_not(has_hi))
     def _():
@@ -204,6 +215,7 @@
         for i in range(6):
             halo1[i, 1] = jnp.zeros((half, half), F32)
         halo_reg[1] = jnp.zeros((nxy, nxy), jnp.int32)
+        far_reg[1] = jnp.zeros((nxy, nxy), jnp.int32)
 
     density = partials[0].astype(F32)
     for g in range(1, partials.shape[0]):
@@ -304,23 +316,48 @@
 
     share(gk, 1)
 
-    recv_reg()
-    e_lo = jnp.where(has_lo, dielectric(halo_reg[0]), e[0])
-    e_hi = jnp.where(has_hi, dielectric(halo_reg[1]), e[1])
-    faces_z = [face(e_lo, e[0], 1.0), face(e[0], e[1], 1.0), face(e[1], e_hi, 1.0)]
-    for i in range(3):
-        fz0[i] = faces_z[i]
+    totals = []
+    middle = face(e[0], e[1], 1.0)
+    fz0[1] = middle
+    part = []
     for p in range(2):
         fx, fy, total = plane_faces(e[p], 1.0)
         fx0[p] = fx
         fy0[p] = fy
-        total = total + faces_z[p] + faces_z[p + 1] + k[p]
+        totals.append(total + middle + k[p])
+        part.append(plane_sum(fx, fy, previous[p]) + middle * previous[1 - p])
+    recv_reg()
+    e_side = [jnp.where(has_lo, dielectric(halo_reg[0]), e[0]),
+              jnp.where(has_hi, dielectric(halo_reg[1]), e[1])]
+    for p in range(2):
+        outer = face(e_side[p], e[p], 1.0)
+        fz0[2 * p] = outer
+        total = totals[p] + outer
         dg0[p] = total
         wt0[p] = DAMPING / total
 
     def beside0(p, mine, below, above):
         return plane_sum(fx0[p], fy0[p], mine) + fz0[p] * below + fz0[p + 1] * above
 
+    def sweep0(p, mine, below, above):
+        return (1.0 - DAMPING) * mine + wt0[p] * (b0[p] + beside0(p, mine, below, above))
+
+    recv_v0()
+    for p in range(2):
+        v1[p] = (1.0 - DAMPING) * previous[p] + wt0[p] * (part[p] + fz0[2 * p] * halo0[0, p])
+
+    got[me] = dens[me]
+    all_in(got, many_recv, 0)
+    for p in range(2):
+        if rows % 8 == 0:
+            b0[p] = got[:, p].reshape(nxy, nxy)
+        else:
+            for s in range(n):
+                b0[p, s * rows:(s + 1) * rows, :] = got[s, p]
+    for p in range(2):
+        v1[p] = v1[p] + wt0[p] * b0[p]
+    recv = launch(v1.at[0], v1.at[1], halo0.at[1], big_send, big_recv, V1)
+    recv_gk = relay(gk, 1)
     recv_e1()
     sz1 = sx1 = 4.0
     fx1, fy1, total1 = plane_faces(e1, sx1)
@@ -329,30 +366,6 @@
     dg1 = total1 + fz1lo + fz1hi + k1
     wt1 = DAMPING / dg1
 
-    def sweep0(p, mine, below, above):
-        return (1.0 - DAMPING) * mine + wt0[p] * (b0[p] + beside0(p, mine, below, above))
-
-    recv_v0()
-    previous_planes = [previous[0], previous[1]]
-    part = [
-        (1.0 - DAMPING) * previous_planes[0]
-        + wt0[0] * beside0(0, previous_planes[0], halo0[0, 0], previous_planes[1]),
-        (1.0 - DAMPING) * previous_planes[1]
-        + wt0[1] * beside0(1, previous_planes[1], previous_planes[0], halo0[0, 1])]
-    for p in range(2):
-        v1[p] = part[p]
-
-    got[me] = dens[me]
-    all_in(got, many_recv, 0)
-    for p in range(2):
-        if rows % 8 == 0:
-            b0[p] = got[:, p].reshape(nxy, nxy)
-        else:
-            for s in range(n):
-                b0[p, s * rows:(s + 1) * rows, :] = got[s, p]
-    for p in range(2):
-        v1[p] = v1[p] + wt0[p] * b0[p]
-    recv = launch(v1.at[0], v1.at[1], halo0.at[1], big_send, big_recv, V1)
     recv()
     v2[0] = sweep0(0, v1[0], halo0[1, 0], v1[1])
     v2[1] = sweep0(1, v1[1], v1[0], halo0[1, 1])
@@ -363,7 +376,11 @@
     r0 = b0[0] - dg0[0] * v2[0] + plane_sum(fx0[0], fy0[0], v2[0]) + fz0[1] * v2[1]
     r1 = b0[1] - dg0[1] * v2[1] + plane_sum(fx0[1], fy0[1], v2[1]) + fz0[1] * v2[0]
     b1 = down0(r0, r1)
-    recv_gk = relay(gk, 1)
+    recv_far = launch(regions.at[1], regions.at[0], far_reg, big_send, big_recv, FAR)
+    recv_gk()
+    e2 = 0.5 * (gk[0] + gk[1]).reshape(n // 2 * quarter, LANES)
+    k2 = back(e2, 1, LANES // 2)
+    coarse = coarse_cycle(e2, k2, n // 2, quarter, 16.0, 16.0)
     recv_term()
     b1 = b1 + halo1[TERM, 0] + halo1[TERM, 1]
 
@@ -381,16 +398,27 @@
     full = down1(b1 - dg1 * a + beside1(a, A2))
     gb[core, chip] = full[:quarter // 2] + back(full[quarter // 2:], 1, LANES // 2)
     share(gb, 2)
-    recv_gk()
-    e2 = 0.5 * (gk[0] + gk[1]).reshape(n // 2 * quarter, LANES)
-    k2 = back(e2, 1, LANES // 2)
-    relay(gb, 2)()
+    recv_v2()
+    base[0] = sweep0(0, v2[0], halo0[2, 0], v2[1])
+    base[1] = sweep0(1, v2[1], v2[0], halo0[2, 1])
+    recv_base = launch(base.at[0], base.at[1], halo0.at[3], big_send, big_recv, BASE)
+    relay_gb = relay(gb, 2)
+    recv_far()
+    for p in range(2):
+        region = halo_reg[p]
+        beyond = face(e_side[p], dielectric(far_reg[p]), 1.0)
+        fx, fy, total = plane_faces(e_side[p], 1.0)
+        fxh[p] = fx
+        fyh[p] = fy
+        fzh[p] = beyond
+        wth[p] = DAMPING / (total + beyond + fz0[2 * p] + jnp.where(region == 2, SCREEN, 0.0))
+    relay_gb()
     packed = 0.5 * (gb[0] + gb[1]).reshape(n // 2 * quarter // 2, LANES)
     split = (n // 2, quarter // 2, LANES)
     b2 = jnp.concatenate(
         [packed.reshape(split), back(packed, 1, LANES // 2).reshape(split)], axis=1
     ).reshape(n // 2 * quarter, LANES)
-    c2 = coarse_cycle(b2, e2, k2, n // 2, quarter, 16.0, 16.0)
+    c2 = coarse(b2)
 
     for i in range(n // 2):
         c2_planes[i] = c2[i * quarter:(i + 1) * quarter]
@@ -412,17 +440,19 @@
     def up0(c):
         return dot(big_l, dot(c, big_r))
 
-    recv_v2()
     mine = up0(a)
-    below = halo0[2, 0] + up0(halo1[A4, 0])
-    above = halo0[2, 1] + up0(halo1[A4, 1])
-    w0, w1 = v2[0] + mine, v2[1] + mine
-    v3[0] = sweep0(0, w0, below, w1)
-    v3[1] = sweep0(1, w1, w0, above)
-    recv = launch(v3.at[0], v3.at[1], halo0.at[3], big_send, big_recv, V3)
-    recv()
-    out[0] = sweep0(0, v3[0], halo0[3, 0], v3[1])
-    out[1] = sweep0(1, v3[1], v3[0], halo0[3, 1])
+    recv_base()
+    v3, side = [], []
+    present = [has_lo, has_hi]
+    for p in range(2):
+        c = up0(halo1[A4, p])
+        own = plane_sum(fx0[p], fy0[p], mine) + fz0[1] * mine + fz0[2 * p] * c
+        v3.append(base[p] + (1.0 - DAMPING) * mine + wt0[p] * own)
+        other = plane_sum(fxh[p], fyh[p], c) + fzh[p] * c + fz0[2 * p] * mine
+        swept = halo0[3, p] + (1.0 - DAMPING) * c + wth[p] * other
+        side.append(jnp.where(present[p], swept, 0.0))
+    out[0] = sweep0(0, v3[0], side[0], v3[1])
+    out[1] = sweep0(1, v3[1], v3[0], side[1])
 
     for sent in pending:
         sent()
@@ -445,11 +475,13 @@
             vmem(n, 2, rows, nxy), vmem(n, 2, rows, nxy), vmem(2, nxy, nxy),
             vmem(2, nxy, nxy), vmem(2, nxy, nxy), vmem(3, nxy, nxy), vmem(2, nxy, nxy),
             vmem(2, nxy, nxy),
-            pltpu.VMEM((2, nxy, nxy), jnp.int32), vmem(4, 2, nxy, nxy),
+            pltpu.VMEM((2, nxy, nxy), jnp.int32), pltpu.VMEM((2, nxy, nxy), jnp.int32),
+            vmem(2, nxy, nxy), vmem(2, nxy, nxy), vmem(2, nxy, nxy), vmem(2, nxy, nxy),
+            vmem(4, 2, nxy, nxy),
             vmem(2, nxy, nxy), vmem(2, nxy, nxy), vmem(2, nxy, nxy),
             vmem(6, 2, half, half), vmem(5, half, half), vmem(2, half, half),
             vmem(2, n // 2, quarter // 2, LANES), vmem(2, n // 2, quarter, LANES),
-            pltpu.SemaphoreType.DMA((5, 2)), pltpu.SemaphoreType.DMA((5, 2)),
+            pltpu.SemaphoreType.DMA((6, 2)), pltpu.SemaphoreType.DMA((6, 2)),
             pltpu.SemaphoreType.DMA((6, 2)), pltpu.SemaphoreType.DMA((6, 2)),
             pltpu.SemaphoreType.DMA((5,)), pltpu.SemaphoreType.DMA((5,)),
             vmem(n // 2, quarter, LANES),

time: 83.3 us -> 80.7 us (0.969)
  Pallas kernels: 81.2 us -> 78.7 us
    pallas_call x1, Pallas kernels: 81.2 us -> 78.7 us  [local(): pl.pallas_call(functools.partial(kernel, n), out_shape=jax.ShapeDtypeStru...]
where the time goes in v3:
time: 80.7 us; the launch traced here: 80.5 us
  Pallas kernels  78.7 us (98%)
  local copies, waits for them, and re-layouts  1.87 us (2%)
    pallas_call x1, Pallas kernels, local(): pl.pallas_call(functools.partial(kernel, n), out_shape=jax.ShapeDtypeStru...  78.7 us
    unnamed x1, local copies, waits for them, and re-layouts  1.87 us

profile of v3, /device:TPU:9, one launch (start us, length us, event | category | flops | bytes accessed | tf_op | source)
XLA Modules:
  0.0 80.5 jit_solution(17728118322390456801)
XLA Ops:
  0.0 78.7 %shard_map.37 = f32[2,256,256]{2,1,0:T(8,128)} custom-call(bf16[4,32,16,256]{3,2,1,0:T(8,128)(2,1)} %partials.1, s32[2,256,256]{2,1,0:T(8,128)} %regions.1, f32[2,256,256]{2,1,0:T(8,128)} %previous.1), custom_call_target="tpu_custom_call" | custom-call | tf_op jit(solution)/shard_map/pallas_call | solution.py:469
  78.7 1.9 %copy.5 = f32[2,256,256]{2,1,0:T(8,128)} copy(f32[2,256,256]{2,1,0:T(8,128)} %shard_map.37) | data formatting | bytes 1048576

commit v4 on v3

--- a/solution.py
+++ b/solution.py
@@ -37,10 +37,26 @@
     return pltpu.roll(v, v.shape[dim] - by, dim)
 
 
-def dot(a, b):
-    return lax.dot_general(
-        a, b, (((1,), (0,)), ((), ())),
-        precision=lax.Precision.HIGHEST, preferred_element_type=F32)
+def terms(v):
+    result = []
+    for _ in range(3):
+        result.append(v.astype(jnp.bfloat16))
+        v = v - result[-1].astype(F32)
+    return result
+
+
+def product(a, b):
+    return lax.dot_general(a, b, (((1,), (0,)), ((), ())), preferred_element_type=F32)
+
+
+def times(v, selector):
+    high, middle, low = (product(t, selector.astype(jnp.bfloat16)) for t in terms(v))
+    return high + (middle + low)
+
+
+def dot(selector, v):
+    high, middle, low = (product(selector.astype(jnp.bfloat16), t) for t in terms(v))
+    return high + (middle + low)
 
 
 def pool_right(wide, narrow, valid):
@@ -145,13 +161,13 @@
 
     def coarsen(f):
         if halve:
-            f = dot(f, right)
+            f = times(f, right)
         parts = [dot(down, f[i:i + part]) for i in range(0, rows, part)]
         return scale * (parts[0] if len(parts) == 1 else jnp.concatenate(parts, axis=0))
 
     def refine(f):
         if halve:
-            f = dot(f, left)
+            f = times(f, left)
         parts = [dot(up, f[i:i + part2]) for i in range(0, rows2, part2)]
         return parts[0] if len(parts) == 1 else jnp.concatenate(parts, axis=0)
 
@@ -276,10 +292,10 @@
     right1, left1 = pool_right(half, LANES, half), pool_left(quarter, half)
 
     def down0(a, b):
-        return 0.125 * dot(left0, dot(a + b, right0))
+        return 0.125 * dot(left0, times(a + b, right0))
 
     def down1(a):
-        return 0.25 * dot(left1, dot(a, right1))
+        return 0.25 * dot(left1, times(a, right1))
 
     e1, k1 = down0(e[0], e[1]), down0(k[0], k[1])
     plane1[E1] = e1
@@ -369,8 +385,8 @@
     recv()
     v2[0] = sweep0(0, v1[0], halo0[1, 0], v1[1])
     v2[1] = sweep0(1, v1[1], v1[0], halo0[1, 1])
-    term1[0] = 0.125 * dot(left0, dot(fz0[0] * v2[0], right0))
-    term1[1] = 0.125 * dot(left0, dot(fz0[2] * v2[1], right0))
+    term1[0] = 0.125 * dot(left0, times(fz0[0] * v2[0], right0))
+    term1[1] = 0.125 * dot(left0, times(fz0[2] * v2[1], right0))
     recv_term = launch(term1.at[0], term1.at[1], halo1.at[TERM], small_send, small_recv, TERM)
     recv_v2 = launch(v2.at[0], v2.at[1], halo0.at[2], big_send, big_recv, V2)
     r0 = b0[0] - dg0[0] * v2[0] + plane_sum(fx0[0], fy0[0], v2[0]) + fz0[1] * v2[1]
@@ -425,7 +441,7 @@
     grow_l, grow_r = spread_left(half, quarter), spread_right(LANES, half, half)
 
     def up1(index):
-        return dot(grow_l, dot(c2_planes[index // 2], grow_r))
+        return dot(grow_l, times(c2_planes[index // 2], grow_r))
 
     halo1[A2, 0] = halo1[A2, 0] + jnp.where(has_lo, up1(jnp.maximum(me - 1, 0)), 0.0)
     halo1[A2, 1] = halo1[A2, 1] + jnp.where(has_hi, up1(jnp.minimum(me + 1, n - 1)), 0.0)
@@ -438,7 +454,7 @@
     big_l, big_r = spread_left(nxy, half), spread_right(half, nxy, nxy)
 
     def up0(c):
-        return dot(big_l, dot(c, big_r))
+        return dot(big_l, times(c, big_r))
 
     mine = up0(a)
     recv_base()

time: 80.7 us -> 78.2 us (0.969)
  Pallas kernels: 78.7 us -> 76.1 us
    pallas_call x1, Pallas kernels: 78.7 us -> 76.1 us  [local(): pl.pallas_call(functools.partial(kernel, n), out_shape=jax.ShapeDtypeStru...]
where the time goes in v4:
time: 78.2 us; the launch traced here: 78 us
  Pallas kernels  76.1 us (97%)
  local copies, waits for them, and re-layouts  1.87 us (2%)
    pallas_call x1, Pallas kernels, local(): pl.pallas_call(functools.partial(kernel, n), out_shape=jax.ShapeDtypeStru...  76.1 us
    unnamed x1, local copies, waits for them, and re-layouts  1.87 us

profile of v4, /device:TPU:9, one launch (start us, length us, event | category | flops | bytes accessed | tf_op | source)
XLA Modules:
  0.0 78.0 jit_solution(13632433643681684353)
XLA Ops:
  0.0 76.1 %shard_map.37 = f32[2,256,256]{2,1,0:T(8,128)} custom-call(bf16[4,32,16,256]{3,2,1,0:T(8,128)(2,1)} %partials.1, s32[2,256,256]{2,1,0:T(8,128)} %regions.1, f32[2,256,256]{2,1,0:T(8,128)} %previous.1), custom_call_target="tpu_custom_call" | custom-call | tf_op jit(solution)/shard_map/pallas_call | solution.py:485
  76.1 1.9 %copy.5 = f32[2,256,256]{2,1,0:T(8,128)} copy(f32[2,256,256]{2,1,0:T(8,128)} %shard_map.37) | data formatting | bytes 1048576
